TPU v7x, 32 devices: a whole 2x2x4 slice. The times are simulated.
32 devices in a mesh: paths: 2 (over x), hi: 16 (over z, y, core).
Axes of the slice: x: 2, y: 2, z: 4, core: 2. Of those that a mesh axis runs over, the one named last changes fastest.
Arguments:
- amplitudes: float32 [2, 2097152], P(None, ('paths', 'hi')), parts along dimension 1, may hold values from -6 to 6
- gate_matrices: bfloat16 [6, 2, 128, 128], replicated, may hold values from -0.375 to 0.375
- phase_qubits: int32 [12, 8, 2], P('paths'), parts along dimension 0, may hold values from 0 to 19
- phase_angles: float32 [12, 8], P('paths'), parts along dimension 0, may hold values from -3.140625 to 3.140625
- cut_qubits: int32 [12, 2], P('paths'), parts along dimension 0, may hold values from 0 to 19
- cut_angle: float32 [12], P('paths'), parts along dimension 0, may hold values from 0.6 to 0.97
- path_index: int32 [12], P('paths'), parts along dimension 0, may hold values from 0 to 1
Outputs:
- final_state: float32 [2, 2097152], P(None, ('paths', 'hi')), parts along dimension 1
There are 2 independent parts, one for each index of `paths`. A program takes and returns all parts, laid end to end along the dimension named above; an argument that names none is the same for every part. Nothing has to cross between parts.
All inputs are finite; a program needn't handle non-finite values.
Results may differ from a plain program's by a relative error of at most 0.0003.
Values sent between devices are 32-bit elements; how exact they have to be, the bound alone decides.
A program may use at most 64 MiB of HBM per device.

v0:
```python
import functools
import math

import jax
import jax.numpy as jnp
from jax import lax
from jax.experimental import pallas as pl
from jax.experimental.pallas import tpu as pltpu
from jax.sharding import PartitionSpec as P

LANES = 128
SUB = 8
MESH = pl.DeviceIdType.MESH


def quarter_sincos(turns):
    whole = jnp.floor(turns + 0.5)
    rest = turns - whole
    square = rest * rest
    half_pi = math.pi / 2
    sin_terms = [(-1) ** k * half_pi ** (2 * k + 1) / math.factorial(2 * k + 1) for k in range(5)]
    cos_terms = [(-1) ** k * half_pi ** (2 * k) / math.factorial(2 * k) for k in range(6)]
    sine = jnp.full_like(square, sin_terms[-1])
    for term in sin_terms[-2::-1]:
        sine = sine * square + term
    sine = sine * rest
    cosine = jnp.full_like(square, cos_terms[-1])
    for term in cos_terms[-2::-1]:
        cosine = cosine * square + term
    count = whole.astype(jnp.int32)
    odd = (count & 1) == 1
    sin_out = jnp.where(odd, cosine, sine)
    cos_out = jnp.where(odd, sine, cosine)
    sin_out = jnp.where((count & 2) == 2, -sin_out, sin_out)
    cos_out = jnp.where(((count + 1) & 2) == 2, -cos_out, cos_out)
    return sin_out, cos_out


def swap_half(value):
    return pltpu.roll(value, LANES // 2, axis=1)


def spread(value, moves):
    total = None
    for a, b in moves:
        term = ((value >> a) & 1) << b
        total = term if total is None else total + term
    return total


def circuit_kernel(
    g, local_bits, layers, pairs, cuts,
    amp_ref, gate_ref, qubit_ref, angle_ref, cut_qubit_ref, cut_angle_ref, path_ref,
    out_ref, recv, weights, gates, cos_all, sin_all, turned,
    send_sem, recv_sem, own_sem, gate_sem,
):
    n = 2**g
    block_bits = local_bits - g - 7
    chunks = 2 ** (block_bits - 3)
    piece = 2 * SUB
    rows = n * SUB
    me = lax.axis_index("hi")
    order = sorted(range(1, n), key=lambda off: abs(off - n // 2))

    def block_rows(owner, chunk):
        return pl.ds(pl.multiple_of((owner * chunks + chunk) * piece, piece), piece)

    def slot_rows(source):
        return pl.ds(pl.multiple_of(source * piece, piece), piece)

    def remote(chunk, off):
        peer = lax.rem(me + off, n)
        return pltpu.make_async_remote_copy(
            src_ref=amp_ref.at[block_rows(peer, chunk)],
            dst_ref=recv.at[chunk, slot_rows(me)],
            send_sem=send_sem.at[chunk, off],
            recv_sem=recv_sem.at[chunk, off],
            device_id={"hi": peer},
            device_id_type=MESH,
        )

    def own(chunk):
        return pltpu.make_async_copy(
            amp_ref.at[block_rows(me, chunk)], recv.at[chunk, slot_rows(me)], own_sem.at[chunk]
        )

    gate_copy = pltpu.make_async_copy(gate_ref, gates, gate_sem)
    gate_copy.start()

    barrier = pltpu.get_barrier_semaphore()
    for off in order:
        pl.semaphore_signal(
            barrier, inc=1, device_id={"hi": lax.rem(me + off, n)}, device_id_type=MESH
        )
    pl.semaphore_wait(barrier, n - 1)

    @pl.loop(0, chunks)
    def _(chunk):
        for off in order:
            remote(chunk, off).start()
        own(chunk).start()

    gate_copy.wait()
    low_lanes = lax.broadcasted_iota(jnp.int32, (64, LANES), 1) < 64

    @pl.loop(0, layers)
    def _(layer):
        real_t = gates[layer, 0].astype(jnp.float32).T
        imag_t = gates[layer, 1].astype(jnp.float32).T
        for t in range(2):
            real_rows = real_t[t * 64 : (t + 1) * 64]
            imag_rows = imag_t[t * 64 : (t + 1) * 64]
            real_turned, imag_turned = swap_half(real_rows), swap_half(imag_rows)
            parts = (
                (
                    jnp.where(low_lanes, real_rows, imag_turned),
                    jnp.where(low_lanes, real_turned, imag_rows),
                ),
                (
                    jnp.where(low_lanes, -imag_rows, real_turned),
                    jnp.where(low_lanes, -imag_turned, real_rows),
                ),
            )
            for c in range(2):
                for t_out in range(2):
                    weights[
                        layer,
                        t * 128 + c * 64 : t * 128 + c * 64 + 64,
                        t_out * 128 : t_out * 128 + 128,
                    ] = parts[c][t_out].astype(jnp.bfloat16)

    def chunk_row(k):
        return block_bits + 3 + k if 10 + k < 7 + g else 3 + k

    lane = lax.broadcasted_iota(jnp.int32, (n, SUB, LANES), 2)
    first = lax.broadcasted_iota(jnp.int32, (n, SUB, LANES), 0)
    second = lax.broadcasted_iota(jnp.int32, (n, SUB, LANES), 1)
    flat_low = lax.broadcasted_iota(jnp.int32, (rows, LANES), 1) < 64
    to_quarter = 2.0 / math.pi

    def entry_index(layer, chunk):
        def place(q):
            if 7 <= q <= 7 + layer:
                return q - 7 + local_bits
            if local_bits <= q <= local_bits + layer:
                return q - local_bits + 7
            return q

        scalar = spread(chunk, [(k, place(10 + k)) for k in range(block_bits - 3)]) + spread(
            me, [(k, place(local_bits - g + k)) for k in range(g)]
        )
        return (
            (lane + spread(second, [(k, place(7 + k)) for k in range(3)]) + scalar)
            + spread(first, [(k, place(local_bits + k)) for k in range(g)])
        )

    def final_index(chunk):
        low_part = lax.broadcasted_iota(jnp.int32, (SUB, n, LANES), 0)
        source = lax.broadcasted_iota(jnp.int32, (SUB, n, LANES), 1)
        lane_part = lax.broadcasted_iota(jnp.int32, (SUB, n, LANES), 2)
        scalar = spread(chunk, [(k, 7 + chunk_row(k)) for k in range(block_bits - 3)])
        return lane_part + (source << 7) + (low_part << (7 + block_bits)) + (
            scalar + (me << local_bits)
        )

    cut_mask = jnp.int32(0)
    cut_turns = jnp.float32(0)
    cut_size = jnp.full((SUB, LANES), 1.0, jnp.float32)
    for k in range(cuts):
        kept = path_ref[k] == 0
        bits = (jnp.int32(1) << cut_qubit_ref[k, 0]) ^ (jnp.int32(1) << cut_qubit_ref[k, 1])
        cut_mask = cut_mask ^ jnp.where(kept, 0, bits)
        cut_turns = cut_turns - jnp.where(kept, 0.0, 1.0)
        sine, cosine = quarter_sincos(
            jnp.full((SUB, LANES), cut_angle_ref[k], jnp.float32) * to_quarter
        )
        kept_all = jnp.full((SUB, LANES), path_ref[k], jnp.int32) == 0
        cut_size = cut_size * jnp.where(kept_all, cosine, sine)

    for layer in range(layers):
        masks = []
        for k in range(pairs):
            mask = (jnp.int32(1) << qubit_ref[layer, k, 0]) | (
                jnp.int32(1) << qubit_ref[layer, k, 1]
            )
            masks.append((mask, angle_ref[layer, k] * to_quarter))

        @pl.loop(0, chunks)
        def _(chunk):
            index = entry_index(layer, chunk) if layer < g else final_index(chunk)
            index = index.reshape(rows, LANES)
            turns = jnp.zeros((rows, LANES), jnp.float32)
            for mask, angle in masks:
                turns = turns + jnp.where((index & mask) == mask, angle, 0.0)
            if layer == 0:
                folded = index & cut_mask
                for shift in (16, 8, 4, 2, 1):
                    folded = folded ^ (folded >> shift)
                turns = turns + cut_turns + ((folded & 1) * 2).astype(jnp.float32)
            sine, cosine = quarter_sincos(turns)
            if layer == 0:
                size = jnp.broadcast_to(cut_size[None], (n, SUB, LANES)).reshape(rows, LANES)
                sine, cosine = sine * size, cosine * size
            sine_turned, cosine_turned = swap_half(sine), swap_half(cosine)
            cos_all[layer, chunk, 0] = jnp.where(flat_low, cosine, cosine_turned)
            cos_all[layer, chunk, 1] = jnp.where(flat_low, cosine_turned, cosine)
            sin_all[layer, chunk, 0] = jnp.where(flat_low, -sine, sine_turned)
            sin_all[layer, chunk, 1] = jnp.where(flat_low, -sine_turned, sine)

    def layer_step(state, layer, chunk, outer, inner):
        shaped = state.reshape(2, outer, 2, inner, LANES)
        joined = jnp.concatenate(
            (shaped[:, :, 0].reshape(rows, LANES), shaped[:, :, 1].reshape(rows, LANES)), axis=1
        )
        high = joined.astype(jnp.bfloat16)
        rest = (joined - high.astype(jnp.float32)).astype(jnp.bfloat16)
        gate = weights[layer]
        product = jnp.dot(high, gate, preferred_element_type=jnp.float32) + jnp.dot(
            rest, gate, preferred_element_type=jnp.float32
        )
        back = jnp.stack(
            (
                product[:, :LANES].reshape(2, outer, inner, LANES),
                product[:, LANES:].reshape(2, outer, inner, LANES),
            ),
            axis=2,
        ).reshape(2 * rows, LANES)
        cosine = cos_all[layer, chunk].reshape(2 * rows, LANES)
        sine = sin_all[layer, chunk].reshape(2 * rows, LANES)
        return back * cosine + swap_half(back) * sine

    @pl.loop(0, chunks)
    def _(chunk):
        own(chunk).wait()
        for off in order:
            remote(chunk, off).wait_recv()
        real = recv[chunk, pl.ds(0, rows, stride=2), :]
        imag = recv[chunk, pl.ds(1, rows, stride=2), :]
        state = jnp.concatenate(
            (
                jnp.where(flat_low, real, swap_half(imag)),
                jnp.where(flat_low, swap_half(real), imag),
            ),
            axis=0,
        )
        for layer in range(g):
            state = layer_step(state, layer, chunk, 2 ** (g - 1 - layer), 2**layer * SUB)
        turned[...] = state
        state = jnp.concatenate(
            [
                turned[pl.ds(b * rows + low, n, stride=SUB), :]
                for b in range(2)
                for low in range(SUB)
            ],
            axis=0,
        )
        for layer in range(g, layers):
            k = layer - g
            state = layer_step(state, layer, chunk, 2 ** (2 - k), 2**k * n)
        zero, one = state[:rows], state[rows:]
        real = jnp.where(flat_low, zero, swap_half(one))
        imag = jnp.where(flat_low, swap_half(zero), one)
        base = spread(chunk, [(k, chunk_row(k)) for k in range(block_bits - 3)])
        for low in range(SUB):
            start = pl.multiple_of(2 * (base + (low << block_bits)), 2 * n)
            out_ref[pl.ds(start, n, stride=2), :] = real[low * n : (low + 1) * n]
            out_ref[pl.ds(start + 1, n, stride=2), :] = imag[low * n : (low + 1) * n]

    @pl.loop(0, chunks)
    def _(chunk):
        for off in order:
            remote(chunk, off).wait_send()


def one_exchange(
    amplitudes, gate_matrices, phase_qubits, phase_angles, cut_qubits, cut_angle, path_index
):
    g = lax.axis_size("hi").bit_length() - 1
    amp_count = amplitudes.shape[1]
    local_bits = amp_count.bit_length() - 1
    layers, pairs = phase_angles.shape
    cuts = cut_angle.shape[0]
    n = 2**g
    chunks = 2 ** (local_bits - g - 10)
    rows = n * SUB
    all_rows = amp_count // LANES
    whole = amplitudes.reshape(2, all_rows, LANES).transpose(1, 0, 2).reshape(2 * all_rows, LANES)
    smem = pl.BlockSpec(memory_space=pltpu.SMEM)
    hbm = pl.BlockSpec(memory_space=pl.ANY)
    result = pl.pallas_call(
        functools.partial(circuit_kernel, g, local_bits, layers, pairs, cuts),
        out_shape=jax.ShapeDtypeStruct((2 * all_rows, LANES), jnp.float32),
        in_specs=[hbm, hbm, smem, smem, smem, smem, smem],
        out_specs=pl.BlockSpec(memory_space=pltpu.VMEM),
        scratch_shapes=[
            pltpu.VMEM((chunks, 2 * rows, LANES), jnp.float32),
            pltpu.VMEM((layers, 256, 256), jnp.bfloat16),
            pltpu.VMEM(gate_matrices.shape, jnp.bfloat16),
            pltpu.VMEM((layers, chunks, 2, rows, LANES), jnp.float32),
            pltpu.VMEM((layers, chunks, 2, rows, LANES), jnp.float32),
            pltpu.VMEM((2 * rows, LANES), jnp.float32),
            pltpu.SemaphoreType.DMA((chunks, n)),
            pltpu.SemaphoreType.DMA((chunks, n)),
            pltpu.SemaphoreType.DMA((chunks,)),
            pltpu.SemaphoreType.DMA,
        ],
        compiler_params=pltpu.CompilerParams(collective_id=0, has_side_effects=True),
    )(whole, gate_matrices, phase_qubits, phase_angles, cut_qubits, cut_angle, path_index)
    return result.reshape(all_rows, 2, LANES).transpose(1, 0, 2).reshape(2, amp_count)


def from_partner(value, axis, bit):
    return lax.ppermute(value, axis, [(i, i ^ 1 << bit) for i in range(lax.axis_size(axis))])


def real_form(matrix):
    real_part = matrix[0].astype(jnp.float32)
    imag_part = matrix[1].astype(jnp.float32)
    upper_rows = jnp.stack((real_part, -imag_part), axis=1)
    lower_rows = jnp.stack((imag_part, real_part), axis=1)
    stacked = jnp.stack((upper_rows, lower_rows), axis=0)
    return stacked.reshape(2, 2, 64, 2, 2, 64)


def apply_gate(amps_now, matrix, target, local_bits):
    shaped = amps_now.reshape(2, 2 ** (local_bits - 1 - target), 2, 2 ** (target - 7), 2, 64)
    result = jnp.einsum(
        "wxyzbd,zabced->waxcey", real_form(matrix), shaped, precision=lax.Precision.HIGHEST
    )
    return result.reshape(2, -1)


def rotate(amps_now, theta):
    cosine = jnp.cos(theta)
    sine = jnp.sin(theta)
    return jnp.stack(
        (cosine * amps_now[0] - sine * amps_now[1], sine * amps_now[0] + cosine * amps_now[1])
    )


def bit_of(index_all, qubit):
    return jnp.bitwise_and(jnp.right_shift(index_all, qubit), 1)


def located(qubit, first_open, global_count, local_bits):
    moved_up = (qubit >= 7 + first_open) & (qubit < 7 + global_count)
    moved_down = (qubit >= local_bits + first_open) & (qubit < local_bits + global_count)
    return jnp.where(
        moved_up, qubit - 7 + local_bits, jnp.where(moved_down, qubit - local_bits + 7, qubit)
    )


def enter_qubit(amps_now, bit_number, local_bits, device_place):
    shaped = amps_now.reshape(2, 2 ** (local_bits - 8 - bit_number), 2, 2**bit_number, 128)
    zero_half = shaped[:, :, 0]
    one_half = shaped[:, :, 1]
    upper_side = jnp.bitwise_and(jnp.right_shift(device_place, bit_number), 1) == 1
    kept_half = jnp.where(upper_side, one_half, zero_half)
    sent_half = jnp.where(upper_side, zero_half, one_half)
    came_half = from_partner(sent_half, "hi", bit_number)
    new_zero = jnp.where(upper_side, came_half, kept_half)
    new_one = jnp.where(upper_side, kept_half, came_half)
    return jnp.stack((new_zero, new_one), axis=2).reshape(2, -1)


def shards(
    amplitudes, gate_matrices, phase_qubits, phase_angles, cut_qubits, cut_angle, path_index
):
    global_count = lax.axis_size("hi").bit_length() - 1
    amp_count = amplitudes.shape[1]
    local_bits = amp_count.bit_length() - 1
    device_place = lax.axis_index("hi")
    index_all = device_place * amp_count + lax.iota(jnp.int32, amp_count)
    layer_count = gate_matrices.shape[0]
    result = amplitudes
    for layer_number in range(layer_count):
        if layer_number < global_count:
            result = enter_qubit(result, layer_number, local_bits, device_place)
            target = 7 + layer_number
        else:
            if layer_number == global_count:
                shaped = result.reshape(2, 2**global_count, 2 ** (local_bits - global_count))
                result = lax.all_to_all(
                    shaped, "hi", split_axis=1, concat_axis=1, tiled=True
                ).reshape(2, -1)
            target = local_bits - 2 * global_count + layer_number
        result = apply_gate(result, gate_matrices[layer_number], target, local_bits)
        theta = jnp.zeros((amp_count,), jnp.float32)
        for pair_number in range(phase_qubits.shape[1]):
            first_pos = located(
                phase_qubits[layer_number, pair_number, 0], global_count, global_count, local_bits
            )
            second_pos = located(
                phase_qubits[layer_number, pair_number, 1], global_count, global_count, local_bits
            )
            both_bits = bit_of(index_all, first_pos) * bit_of(index_all, second_pos)
            theta = theta + phase_angles[layer_number, pair_number] * both_bits.astype(jnp.float32)
        result = rotate(result, theta)
        if layer_number == 0:
            for cut_number in range(cut_qubits.shape[0]):
                first_cut = located(
                    cut_qubits[cut_number, 0], global_count, global_count, local_bits
                )
                second_cut = located(
                    cut_qubits[cut_number, 1], global_count, global_count, local_bits
                )
                parity = jnp.bitwise_xor(
                    bit_of(index_all, first_cut), bit_of(index_all, second_cut)
                )
                signs = (1 - 2 * parity).astype(jnp.float32)
                chosen = path_index[cut_number] == 0
                angle_now = cut_angle[cut_number]
                keep_part = jnp.where(chosen, jnp.cos(angle_now), jnp.zeros_like(angle_now))
                turn_part = jnp.where(chosen, jnp.zeros_like(angle_now), jnp.sin(angle_now))
                result = jnp.stack(
                    (
                        keep_part * result[0] + turn_part * signs * result[1],
                        keep_part * result[1] - turn_part * signs * result[0],
                    )
                )
    return result


def any_slice(amplitudes, gate_matrices, *rest):
    g = lax.axis_size("hi").bit_length() - 1
    local_bits = amplitudes.shape[1].bit_length() - 1
    late_layers = gate_matrices.shape[0] - g
    fits = 3 <= g <= local_bits - g - 7 and local_bits - g >= 11 and 0 < late_layers <= 3
    plan = one_exchange if fits else shards
    return plan(amplitudes, gate_matrices, *rest)


def solution(mesh):
    placed = (
        P(None, ("paths", "hi")),
        P(),
        P("paths", None, None),
        P("paths", None),
        P("paths", None),
        P("paths"),
        P("paths"),
    )
    return jax.shard_map(
        any_slice, mesh=mesh, in_specs=placed, out_specs=P(None, ("paths", "hi")), check_vma=False
    )
```

profile of v0, /device:TPU:0, one launch (start us, length us, event | category | flops | bytes accessed | tf_op | source)
XLA Modules:
  0.0 27.6 jit_solution(5194997530815619154)
XLA Ops:
  0.0 0.0 copy-start
  0.0 1.4 %copy.10.cut_qubit_ref = s32[6,2]{1,0:T(8,128)} copy(s32[6,2]{0,1:T(2,128)} %param.11) | data formatting | bytes 96 | tf_op args[4]
  1.4 0.0 copy-done
  1.4 0.7 %copy.9.qubit_ref = s32[6,8,2]{2,1,0:T(8,128)} copy(s32[6,8,2]{1,2,0:T(2,128)S(1)} %copy-done) | data formatting | bytes 768 | tf_op args[2]
  2.1 23.7 %shard_map.73 = f32[1024,128]{1,0:T(8,128)} custom-call(f32[1024,128]{1,0:T(8,128)} %bitcast.11, bf16[6,2,128,128]{3,2,1,0:T(8,128)(2,1)} %gate_ref.1, s32[6,8,2]{2,1,0:T(8,128)} %copy.9.qubit_ref, f32[6,8]{1,0:T(8,128)} %angle_ref.1, s32[6,2]{1,0:T(8,128)} %copy.10.cut_qubit_ref, f32[6]{0:T(128)} %cut_angle_ref.1, s32[6]{0:T(128)} %path_ref.1), custom_call_target="tpu_custom_call" | custom-call | tf_op jit(solution)/shard_map/pallas_call | solution.py:290
  25.8 1.9 %copy.13 = f32[2,65536]{1,0:T(2,128)} copy(f32[2,65536]{1,0:T(2,128)} %bitcast.10) | data formatting | bytes 1048576
Async XLA Ops:
  0.0 1.4 %copy-start = (s32[6,8,2]{1,2,0:T(2,128)S(1)}, s32[6,8,2]{1,2,0:T(2,128)}, u32[]{:S(2)}) copy-start(s32[6,8,2]{1,2,0:T(2,128)} %param.9) | copy-start | bytes 1156
where the time goes:
time: 27.9 us; the launch traced here: 27.6 us
  Pallas kernels  23.7 us (85%)
  local copies, waits for them, and re-layouts  3.94 us (14%)
    pallas_call x1, Pallas kernels, one_exchange(): pl.pallas_call(functools.partial(circuit_kernel, g, local_bits, layers, p...  23.7 us
    unnamed x5, local copies, waits for them, and re-layouts  3.94 us

commit v1 on v0

--- a/solution.py
+++ b/solution.py
@@ -50,9 +50,10 @@
 
 def circuit_kernel(
     g, local_bits, layers, pairs, cuts,
-    amp_ref, gate_ref, qubit_ref, angle_ref, cut_qubit_ref, cut_angle_ref, path_ref,
-    out_ref, recv, weights, gates, cos_all, sin_all, turned,
-    send_sem, recv_sem, own_sem, gate_sem,
+    amp_ref, gate_ref, qubit_in, angle_in, cut_qubit_in, cut_angle_in, path_in, out_ref,
+    qubit_ref, angle_ref, cut_qubit_ref, cut_angle_ref, path_ref,
+    recv, weights, gates, cos_all, sin_all, turned,
+    send_sem, recv_sem, own_sem, gate_sem, small_sem,
 ):
     n = 2**g
     block_bits = local_bits - g - 7
@@ -86,6 +87,19 @@
 
     gate_copy = pltpu.make_async_copy(gate_ref, gates, gate_sem)
     gate_copy.start()
+    smalls = (
+        (qubit_in, qubit_ref),
+        (angle_in, angle_ref),
+        (cut_qubit_in, cut_qubit_ref),
+        (cut_angle_in, cut_angle_ref),
+        (path_in, path_ref),
+    )
+    small_copies = [
+        pltpu.make_async_copy(source, target, small_sem.at[k])
+        for k, (source, target) in enumerate(smalls)
+    ]
+    for small_copy in small_copies:
+        small_copy.start()
 
     barrier = pltpu.get_barrier_semaphore()
     for off in order:
@@ -163,12 +177,14 @@
             scalar + (me << local_bits)
         )
 
+    for small_copy in small_copies:
+        small_copy.wait()
     cut_mask = jnp.int32(0)
     cut_turns = jnp.float32(0)
     cut_size = jnp.full((SUB, LANES), 1.0, jnp.float32)
     for k in range(cuts):
         kept = path_ref[k] == 0
-        bits = (jnp.int32(1) << cut_qubit_ref[k, 0]) ^ (jnp.int32(1) << cut_qubit_ref[k, 1])
+        bits = (jnp.int32(1) << cut_qubit_ref[0, k]) ^ (jnp.int32(1) << cut_qubit_ref[1, k])
         cut_mask = cut_mask ^ jnp.where(kept, 0, bits)
         cut_turns = cut_turns - jnp.where(kept, 0.0, 1.0)
         sine, cosine = quarter_sincos(
@@ -180,8 +196,8 @@
     for layer in range(layers):
         masks = []
         for k in range(pairs):
-            mask = (jnp.int32(1) << qubit_ref[layer, k, 0]) | (
-                jnp.int32(1) << qubit_ref[layer, k, 1]
+            mask = (jnp.int32(1) << qubit_ref[layer, 0, k]) | (
+                jnp.int32(1) << qubit_ref[layer, 1, k]
             )
             masks.append((mask, angle_ref[layer, k] * to_quarter))
 
@@ -285,14 +301,18 @@
     rows = n * SUB
     all_rows = amp_count // LANES
     whole = amplitudes.reshape(2, all_rows, LANES).transpose(1, 0, 2).reshape(2 * all_rows, LANES)
-    smem = pl.BlockSpec(memory_space=pltpu.SMEM)
-    hbm = pl.BlockSpec(memory_space=pl.ANY)
+    hbm = pl.BlockSpec(memory_space=pltpu.HBM)
     result = pl.pallas_call(
         functools.partial(circuit_kernel, g, local_bits, layers, pairs, cuts),
-        out_shape=jax.ShapeDtypeStruct((2 * all_rows, LANES), jnp.float32),
-        in_specs=[hbm, hbm, smem, smem, smem, smem, smem],
+        out_shape=pltpu.VMEM((2 * all_rows, LANES), jnp.float32),
+        in_specs=[hbm] * 7,
         out_specs=pl.BlockSpec(memory_space=pltpu.VMEM),
         scratch_shapes=[
+            pltpu.SMEM((layers, 2, pairs), jnp.int32),
+            pltpu.SMEM(phase_angles.shape, jnp.float32),
+            pltpu.SMEM((2, cuts), jnp.int32),
+            pltpu.SMEM(cut_angle.shape, jnp.float32),
+            pltpu.SMEM(path_index.shape, jnp.int32),
             pltpu.VMEM((chunks, 2 * rows, LANES), jnp.float32),
             pltpu.VMEM((layers, 256, 256), jnp.bfloat16),
             pltpu.VMEM(gate_matrices.shape, jnp.bfloat16),
@@ -303,9 +323,13 @@
             pltpu.SemaphoreType.DMA((chunks, n)),
             pltpu.SemaphoreType.DMA((chunks,)),
             pltpu.SemaphoreType.DMA,
+            pltpu.SemaphoreType.DMA((5,)),
         ],
         compiler_params=pltpu.CompilerParams(collective_id=0, has_side_effects=True),
-    )(whole, gate_matrices, phase_qubits, phase_angles, cut_qubits, cut_angle, path_index)
+    )(
+        whole, gate_matrices, phase_qubits.transpose(0, 2, 1), phase_angles,
+        cut_qubits.transpose(1, 0), cut_angle, path_index,
+    )
     return result.reshape(all_rows, 2, LANES).transpose(1, 0, 2).reshape(2, amp_count)
 
 

time: 27.9 us -> 22.6 us (0.81)
  local copies, waits for them, and re-layouts: 3.94 us -> 0.8 us
  Pallas kernels: 23.7 us -> 21.7 us
    unnamed x5 -> x1, local copies, waits for them, and re-layouts: 3.94 us -> 0.8 us
    pallas_call x1, Pallas kernels: 23.7 us -> 21.7 us  [one_exchange(): pl.pallas_call(functools.partial(circuit_kernel, g, local_bits, layers, p...]
where the time goes in v1:
time: 22.6 us; the launch traced here: 22.5 us
  Pallas kernels  21.7 us (96%)
  local copies, waits for them, and re-layouts  0.8 us (4%)
    pallas_call x1, Pallas kernels, one_exchange(): pl.pallas_call(functools.partial(circuit_kernel, g, local_bits, layers, p...  21.7 us
    unnamed x1, local copies, waits for them, and re-layouts  0.8 us

profile of v1, /device:TPU:0, one launch (start us, length us, event | category | flops | bytes accessed | tf_op | source)
XLA Modules:
  0.0 22.5 jit_solution(11994239540469251214)
XLA Ops:
  0.0 21.7 %shard_map.73 = f32[1024,128]{1,0:T(8,128)S(1)} custom-call(f32[1024,128]{1,0:T(8,128)} %bitcast.13, bf16[6,2,128,128]{3,2,1,0:T(8,128)(2,1)} %gate_ref.1, s32[6,2,8]{2,1,0:T(2,128)} %bitcast.14, f32[6,8]{1,0:T(8,128)} %angle_in.1, s32[2,6]{1,0:T(2,128)} %bitcast.15, f32[6]{0:T(128)} %cut_angle_in.1, s32[6]{0:T(128)} %path_in.1), custom_call_target="tpu_custom_call" | custom-call | tf_op jit(solution)/shard_map/pallas_call | solution.py:305
  21.7 0.8 %copy.11 = f32[2,65536]{1,0:T(2,128)} copy(f32[2,65536]{1,0:T(2,128)S(1)} %bitcast.12) | data formatting | bytes 1048576

commit v2 on v1

--- a/solution.py
+++ b/solution.py
@@ -61,7 +61,7 @@
     piece = 2 * SUB
     rows = n * SUB
     me = lax.axis_index("hi")
-    order = sorted(range(1, n), key=lambda off: abs(off - n // 2))
+    order = range(1, n)
 
     def block_rows(owner, chunk):
         return pl.ds(pl.multiple_of((owner * chunks + chunk) * piece, piece), piece)
@@ -231,9 +231,10 @@
         high = joined.astype(jnp.bfloat16)
         rest = (joined - high.astype(jnp.float32)).astype(jnp.bfloat16)
         gate = weights[layer]
-        product = jnp.dot(high, gate, preferred_element_type=jnp.float32) + jnp.dot(
-            rest, gate, preferred_element_type=jnp.float32
-        )
+        both = jnp.dot(
+            jnp.concatenate((high, rest), axis=0), gate, preferred_element_type=jnp.float32
+        )
+        product = both[:rows] + both[rows:]
         back = jnp.stack(
             (
                 product[:, :LANES].reshape(2, outer, inner, LANES),

time: 22.6 us -> 22.1 us (0.978)
  Pallas kernels: 21.7 us -> 21.1 us
    pallas_call x1, Pallas kernels: 21.7 us -> 21.1 us  [one_exchange(): pl.pallas_call(functools.partial(circuit_kernel, g, local_bits, layers, p...]
where the time goes in v2:
time: 22.1 us; the launch traced here: 22 us
  Pallas kernels  21.1 us (95%)
  local copies, waits for them, and re-layouts  0.8 us (4%)
    pallas_call x1, Pallas kernels, one_exchange(): pl.pallas_call(functools.partial(circuit_kernel, g, local_bits, layers, p...  21.1 us
    unnamed x1, local copies, waits for them, and re-layouts  0.8 us

profile of v2, /device:TPU:0, one launch (start us, length us, event | category | flops | bytes accessed | tf_op | source)
XLA Modules:
  0.0 22.0 jit_solution(16976542289797530665)
XLA Ops:
  0.0 21.1 %shard_map.73 = f32[1024,128]{1,0:T(8,128)S(1)} custom-call(f32[1024,128]{1,0:T(8,128)} %bitcast.13, bf16[6,2,128,128]{3,2,1,0:T(8,128)(2,1)} %gate_ref.1, s32[6,2,8]{2,1,0:T(2,128)} %bitcast.14, f32[6,8]{1,0:T(8,128)} %angle_in.1, s32[2,6]{1,0:T(2,128)} %bitcast.15, f32[6]{0:T(128)} %cut_angle_in.1, s32[6]{0:T(128)} %path_in.1), custom_call_target="tpu_custom_call" | custom-call | tf_op jit(solution)/shard_map/pallas_call | solution.py:306
  21.2 0.8 %copy.11 = f32[2,65536]{1,0:T(2,128)} copy(f32[2,65536]{1,0:T(2,128)S(1)} %bitcast.12) | data formatting | bytes 1048576
